TPU v7x, 512 devices: a whole 4x4x16 slice. The times are simulated.
512 devices in a mesh: vec: 64 (over x, z_hi, y), orb: 8 (over z_lo, core).
Axes of the slice: x: 4, y: 4, z: 16 (z_hi: 4, z_lo: 4; z = z_hi * 4 + z_lo), core: 2. Of those that a mesh axis runs over, the one named last changes fastest.
Arguments:
- cholesky: bfloat16 [256, 2048, 2048], P('vec', 'orb'), may hold values from -4 to 4
- active_coeff: bfloat16 [2048, 24], replicated, may hold values from -0.125 to 0.125
- pair_density: bfloat16 [24, 24, 576], replicated, may hold values from -0.0546875 to 0.0546875
Outputs:
- active_integrals: float32 [2048, 24, 576], P(('orb', 'vec'))
- general_fock: float32 [2048, 24], P(('orb', 'vec'))
All inputs are finite; a program needn't handle non-finite values.
Results may differ from a plain program's by a relative error of at most 0.0049.
Values may be sent and summed in bfloat16 or wider, within the bound.
A program may use at most 64 MiB of HBM per device.

v0:
```python
import jax
import jax.numpy as jnp
from jax import lax
from jax.sharding import PartitionSpec as P


def shards(cholesky, active_coeff, pair_density):
    vec_count = lax.axis_size("vec")
    orb_pos = lax.axis_index("orb")
    local_vecs, block_rows, basis = cholesky.shape
    n_act = active_coeff.shape[1]
    rows_here = block_rows // vec_count
    half = jnp.einsum(
        "qmn,nu->mqu", cholesky, active_coeff, preferred_element_type=jnp.float32
    ).astype(jnp.bfloat16)
    flat = half.reshape(block_rows, local_vecs * n_act)
    moved = lax.all_to_all(flat, "vec", split_axis=0, concat_axis=1, tiled=True)
    regrouped = moved.reshape(rows_here, -1, n_act)
    coeff_rows = lax.dynamic_slice_in_dim(active_coeff, orb_pos * block_rows, block_rows, 0)
    partial_value = jnp.einsum("mv,mqw->qvw", coeff_rows, half, preferred_element_type=jnp.float32)
    own_sum = lax.psum(partial_value.reshape(local_vecs, n_act * n_act), "orb")
    own_active = own_sum.astype(jnp.bfloat16)
    integrals = jnp.einsum(
        "mqu,qx->mux",
        regrouped,
        lax.all_gather(own_active, "vec", axis=0, tiled=True),
        preferred_element_type=jnp.float32,
    )
    density = pair_density.astype(jnp.float32)
    fock = jnp.dot(
        integrals.reshape(rows_here, -1),
        density.reshape(n_act, -1).T,
        precision=lax.Precision.HIGHEST,
    )
    return (integrals, fock)


def solution(mesh):
    return jax.shard_map(
        shards,
        mesh=mesh,
        in_specs=(P("vec", "orb", None), P(), P()),
        out_specs=(P(("orb", "vec"), None, None), P(("orb", "vec"), None)),
        check_vma=False,
    )
```

profile of v0, /device:TPU:32, one launch (start us, length us, event | category | flops | bytes accessed | tf_op | source)
XLA Modules:
  0.0 276.5 jit_solution(8025990669206017411)
XLA Ops:
  0.6 0.0 copy-start
  0.6 3.5 %fusion = bf16[256,4,24]{0,2,1:T(8,128)(2,1)S(1)} fusion(bf16[4,256,2048]{2,1,0:T(8,128)(2,1)} %param.3, bf16[2048,24]{0,1:T(8,128)(2,1)} %param.4), kind=kOutput, calls=%fused_computation.1 | convolution fusion | flops 100687872 | bytes 4341760 | tf_op jit(solution)/shard_map/qmn,nu->mqu/dot_general | solution.py:13
  4.1 0.2 copy.14
  4.3 0.8 all_to_all.12
  5.2 20.3 %all-to-all-start = ((bf16[64,4,96]{2,1,0:T(4,128)(2,1)}), bf16[64,4,96]{2,1,0:T(4,128)(2,1)S(1)}, u32[]{:S(2)}, u32[]{:S(2)}) async-start(bf16[64,4,96]{2,1,0:T(4,128)(2,1)} %all_to_all.12), calls=%async_computation | async-start | bytes 131072 | tf_op jit(solution)/shard_map/all_to_all | solution.py:17
  25.5 0.8 convolution_bitcast_fusion
  26.3 0.1 copy.16
  26.4 0.1 reshape.19
  26.5 24.4 %psum.7 = bf16[4,576]{1,0:T(4,128)(2,1)S(1)} all-reduce(f32[4,576]{1,0:T(4,128)S(1)} %reshape.19), channel_id=1, replica_groups=mesh['vec'=64,'orb'=8] {'orb'}, use_global_device_ids=true, to_apply=%region_0.0 | all-reduce | flops 2304 | bytes 13824 | tf_op jit(solution)/shard_map/psum | solution.py:21
  50.9 223.6 %all-gather = bf16[64,4,576]{2,1,0:T(4,128)(2,1)S(1)} all-gather(bf16[1,4,576]{2,1,0:T(4,128)(2,1)S(1)} %bitcast.23), channel_id=1, replica_groups=mesh['vec'=64,'orb'=8] {'vec'}, dimensions={0}, use_global_device_ids=true | all-gather | bytes 299520 | tf_op jit(solution)/shard_map/all_gather | solution.py:26
  274.5 0.2 reshape.21
  274.6 0.0 all-to-all-done
  274.7 0.2 reshape.18
  274.8 0.2 fusion.2
  275.1 0.0 copy-done
  275.1 0.0 copy-start.1
  275.1 1.4 convolution_bitcast_fusion.1
  276.5 0.0 copy-done.1
  (1 shorter events, 0.0 us)
Async XLA Ops:
  0.6 274.4 %copy-start = (bf16[24,24,576]{2,1,0:T(8,128)(2,1)S(1)}, bf16[24,24,576]{2,1,0:T(8,128)(2,1)}, u32[]{:S(2)}) copy-start(bf16[24,24,576]{2,1,0:T(8,128)(2,1)} %param.5) | copy-start | bytes 1990660
  5.2 269.5 %all-to-all-start = ((bf16[64,4,96]{2,1,0:T(4,128)(2,1)}), bf16[64,4,96]{2,1,0:T(4,128)(2,1)S(1)}, u32[]{:S(2)}, u32[]{:S(2)}) async-start(bf16[64,4,96]{2,1,0:T(4,128)(2,1)} %all_to_all.12), calls=%async_computation | async-start | bytes 131072 | tf_op jit(solution)/shard_map/all_to_all | solution.py:17
  275.1 1.4 copy-start.1
where the time goes:
time: 277 us
  blocking collectives  248 us (90%)
  starting transfers between devices  20.3 us (7%)
  matrix products  6.01 us (2%)
    all_gather x1, blocking collectives, shards(): lax.all_gather(own_active, 'vec', axis=0, tiled=True)  224 us
    psum x1, blocking collectives, shards(): own_sum = lax.psum(partial_value.reshape(local_vecs, n_act * n_act), 'orb')  24.4 us
    all_to_all x1, starting transfers between devices, shards(): moved = lax.all_to_all(flat, 'vec', split_axis=0, concat_axis=1, tiled=True)  20.3 us
  transfers between devices with their start and end apart: 1, of which 0 were waited for; matrix products, arithmetic and copies ran while one was open for 0% of the time, Pallas kernels for 0%

commit v1 on v0

v1 whole, which is shorter than its diff:
```python
import jax
import jax.numpy as jnp
from jax import lax
from jax.experimental import pallas as pl
from jax.experimental.pallas import tpu as pltpu
from jax.sharding import PartitionSpec as P

MESH = pl.DeviceIdType.MESH
F32 = jnp.float32
BF16 = jnp.bfloat16
NT = (((1,), (1,)), ((), ()))
TN = (((0,), (0,)), ((), ()))


def kernel(
    chol, coeff_t, density, out, fock,
    chol_v, coeff_pad, coeff_blk, density_v, half32, spread, rows_out, rows_in, rows32,
    turn_out, turn_in, turn32, part32, pair_in, part_out, part_in, sum32, block_out, gathered, ints,
    chol_sem, density_sem, pair_send, pair_recv, rows_send, rows_recv, part_send, part_recv,
    turn_send, turn_recv, block_send, block_recv, share_send, share_recv,
):
    vec, orb = lax.axis_index("vec"), lax.axis_index("orb")
    x, zh, y = vec // 16, (vec // 4) % 4, vec % 4
    zl, core = orb // 2, orb % 2

    def plane(k):
        return (((x + k // 4) % 4) * 16 + zh * 4 + (y + k % 4) % 4, orb)

    def column(k):
        return (x * 16 + ((zh + k // 4) % 4) * 4 + y, ((zl + k % 4) % 4) * 2 + core)

    sibling = (vec, zl * 2 + 1 - core)

    def remote(src, dst, send, recv, device):
        return pltpu.make_async_remote_copy(
            src_ref=src, dst_ref=dst, send_sem=send, recv_sem=recv, device_id=device, device_id_type=MESH
        )

    barrier = pltpu.get_barrier_semaphore()
    pl.semaphore_signal(barrier, inc=1, device_id=sibling, device_id_type=MESH)

    @pl.loop(1, 16)
    def _(k):
        pl.semaphore_signal(barrier, inc=1, device_id=column(k), device_id_type=MESH)
        pl.semaphore_signal(barrier, inc=1, device_id=plane(k), device_id_type=MESH)

    def fetch(n):
        piece = (n // 2, pl.ds((n % 2) * 128, 128))
        return pltpu.make_async_copy(chol.at[piece], chol_v.at[piece], chol_sem.at[n])

    for n in range(8):
        fetch(n).start()
    density_copy = pltpu.make_async_copy(density, density_v, density_sem)
    density_copy.start()

    coeff_pad[...] = jnp.zeros_like(coeff_pad)
    coeff_pad[0:24, :] = coeff_t[...]
    for n in range(2):
        lanes = pl.ds(pl.multiple_of(orb * 256 + n * 128, 128), 128)
        coeff_blk[n * 24 : n * 24 + 24, :] = coeff_t[:, lanes].astype(F32)
    coeff_rows = jnp.concatenate(
        [
            jnp.concatenate([coeff_blk[pl.ds(n * 24 + k, 8, stride=3), :] for k in range(3)], axis=0)
            for n in range(2)
        ],
        axis=1,
    ).astype(BF16)

    for q in range(4):
        for n in range(2):
            fetch(2 * q + n).wait()
            rows = lax.dot_general(
                chol_v[q, n * 128 : n * 128 + 128, :], coeff_pad[...], NT, preferred_element_type=F32
            )
            half32[q * 256 + n * 128 : q * 256 + n * 128 + 128, :] = rows.astype(BF16).astype(F32)
        part = jnp.dot(
            coeff_rows, half32[q * 256 : q * 256 + 256, :].astype(BF16), preferred_element_type=F32
        )
        packed = part[0:8] + pltpu.roll(part[8:16], 24, 1) + pltpu.roll(part[16:24], 48, 1)
        part32[0, q * 4 : q * 4 + 4, :] = packed[0:4]
        part32[1, q * 4 : q * 4 + 4, :] = packed[4:8]

    pl.semaphore_wait(barrier, 31)

    pair_copy = remote(part32.at[1 - core], pair_in, pair_send, pair_recv, sibling)
    pair_copy.start()

    for yy in range(4):
        for zz in range(4):
            at = zz * 16 + yy * 4
            group = half32[pl.ds(at, 16, stride=64), :]
            for i in range(1, 4):
                group = group + pltpu.roll(half32[pl.ds(at + i, 16, stride=64), :], 24 * i, 1)
            spread[yy * 64 + zz * 16 : yy * 64 + zz * 16 + 16, :] = group
        for xx in range(4):
            rows_out[xx * 4 + yy] = spread[pl.ds(yy * 64 + xx, 16, stride=4), :].astype(BF16)

    def rows_copy(k):
        to = ((x + k // 4) % 4) * 4 + (y + k % 4) % 4
        return remote(rows_out.at[to], rows_in.at[k], rows_send.at[k], rows_recv.at[k], plane(k))

    @pl.loop(1, 16)
    def _(k):
        rows_copy(k).start()

    pair_copy.wait_recv()
    mine = (part32[core] + pair_in[...]).astype(BF16)
    part_out[...] = mine
    part_in[0] = mine

    def part_copy(k):
        return remote(part_out, part_in.at[k], part_send.at[k], part_recv.at[k], column(k))

    @pl.loop(1, 16)
    def _(k):
        part_copy(k).start()

    rows_in[0] = rows_out[x * 4 + y]

    @pl.loop(1, 16)
    def _(k):
        rows_copy(k).wait_recv()

    for k in range(16):
        rows32[k * 16 : k * 16 + 16, :] = rows_in[k].astype(F32)
    for zz in range(4):
        for q in range(4):
            turn_out[zz, q * 16 : q * 16 + 16, :] = rows32[pl.ds(zz * 4 + q, 16, stride=16), :].astype(BF16)

    def turn_copy(k):
        to = (zh + k) % 4
        device = (x * 16 + to * 4 + y, orb)
        return remote(turn_out.at[to], turn_in.at[k], turn_send.at[k], turn_recv.at[k], device)

    @pl.loop(1, 4)
    def _(k):
        turn_copy(k).start()

    turn_in[0] = turn_out[zh]

    @pl.loop(1, 16)
    def _(k):
        part_copy(k).wait_recv()

    for h in range(4):
        total = part_in[4 * h].astype(F32)
        for n in range(1, 4):
            total = total + part_in[4 * h + n].astype(F32)
        sum32[h * 16 : h * 16 + 16, :] = total
    piece = [sum32[pl.ds(j, 16, stride=4), :] for j in range(4)]
    lane = lax.broadcasted_iota(jnp.int32, (16, 128), 1)
    one, two, three = pltpu.roll(piece[1], 72, 1), pltpu.roll(piece[2], 16, 1), pltpu.roll(piece[3], 88, 1)
    left = (piece[0] + jnp.where(lane >= 72, one, 0.0)).astype(BF16)
    middle = (jnp.where(lane < 16, one, 0.0) + two + jnp.where(lane >= 88, three, 0.0)).astype(BF16)
    right = jnp.where(lane < 32, three, 0.0).astype(BF16)
    for n, tile in enumerate((left, middle, right)):
        block_out[:, n * 128 : n * 128 + 128] = tile
        gathered[core, 0, :, n * 128 : n * 128 + 128] = tile

    def block_copy(k):
        return remote(block_out, gathered.at[core, k], block_send.at[k], block_recv.at[k], plane(k))

    def share_copy(k):
        there = gathered.at[core, k]
        return remote(there, there, share_send.at[k], share_recv.at[k], sibling)

    @pl.loop(1, 16)
    def _(k):
        block_copy(k).start()

    share_copy(0).start()

    @pl.loop(1, 4)
    def _(k):
        turn_copy(k).wait_recv()

    for k in range(4):
        turn32[k * 64 : k * 64 + 64, :] = turn_in[k].astype(F32)
    own = jnp.concatenate([turn32[pl.ds(k, 16, stride=16), :] for k in range(16)], axis=0)
    own = own.astype(BF16)[:, 0:96]

    @pl.loop(1, 16)
    def _(k):
        block_copy(k).wait_recv()
        share_copy(k).start()

    @pl.loop(0, 16)
    def _(k):
        there = gathered.at[1 - core, k]
        remote(there, there, share_send.at[k], share_recv.at[k], sibling).wait_recv()

    first = lax.dot_general(own, gathered[0].reshape(256, 384), TN, preferred_element_type=F32)
    second = lax.dot_general(own, gathered[1].reshape(256, 384), TN, preferred_element_type=F32)
    lane = lax.broadcasted_iota(jnp.int32, (96, 128), 1)
    a, b, c = (pltpu.roll(second[:, n * 128 : n * 128 + 128], 32, 1) for n in range(3))
    tiles = (
        first[:, 0:128],
        first[:, 128:256],
        first[:, 256:384] + jnp.where(lane >= 32, a, 0.0),
        jnp.where(lane < 32, a, b),
        jnp.where(lane < 32, b, c),
    )
    for n, tile in enumerate(tiles):
        width = min(128, 576 - n * 128)
        tile = tile[:, 0:width]
        out[:, :, n * 128 : n * 128 + width] = tile.reshape(4, 24, width)
        high = tile.astype(BF16)
        ints[0:96, n * 128 : n * 128 + width] = high
        ints[96:192, n * 128 : n * 128 + width] = (tile - high.astype(F32)).astype(BF16)

    density_copy.wait()
    pairs = lax.dot_general(ints[...], density_v[...], NT, preferred_element_type=F32)
    pairs = pairs[0:96] + pairs[96:192]
    row = lax.broadcasted_iota(jnp.int32, (96, 576), 0) % 24
    col = lax.broadcasted_iota(jnp.int32, (96, 576), 1) % 24
    kept = jnp.where(row == col, pairs, 0.0).reshape(4, 24, 576).sum(axis=1)
    pick = lax.broadcasted_iota(jnp.int32, (576, 24), 0) // 24 == lax.broadcasted_iota(jnp.int32, (576, 24), 1)
    fock[...] = jnp.dot(kept, pick.astype(F32), precision=lax.Precision.HIGHEST, preferred_element_type=F32)

    pair_copy.wait_send()
    share_copy(0).wait_send()

    @pl.loop(1, 16)
    def _(k):
        rows_copy(k).wait_send()
        part_copy(k).wait_send()
        block_copy(k).wait_send()
        share_copy(k).wait_send()

    @pl.loop(1, 4)
    def _(k):
        turn_copy(k).wait_send()


def shards(cholesky, active_coeff, pair_density):
    vmem = pl.BlockSpec(memory_space=pltpu.VMEM)
    hbm = pl.BlockSpec(memory_space=pl.ANY)
    dma = pltpu.SemaphoreType.DMA
    return pl.pallas_call(
        kernel,
        name="half_active_fock",
        out_shape=(jax.ShapeDtypeStruct((4, 24, 576), F32), jax.ShapeDtypeStruct((4, 24), F32)),
        in_specs=[hbm, vmem, hbm],
        out_specs=(vmem, vmem),
        scratch_shapes=[
            pltpu.VMEM((4, 256, 2048), BF16),
            pltpu.VMEM((128, 2048), BF16),
            pltpu.VMEM((48, 128), F32),
            pltpu.VMEM((576, 576), BF16),
            pltpu.VMEM((1024, 128), F32),
            pltpu.VMEM((256, 128), F32),
            pltpu.VMEM((16, 16, 128), BF16),
            pltpu.VMEM((16, 16, 128), BF16),
            pltpu.VMEM((256, 128), F32),
            pltpu.VMEM((4, 64, 128), BF16),
            pltpu.VMEM((4, 64, 128), BF16),
            pltpu.VMEM((256, 128), F32),
            pltpu.VMEM((2, 16, 128), F32),
            pltpu.VMEM((16, 128), F32),
            pltpu.VMEM((16, 128), BF16),
            pltpu.VMEM((16, 16, 128), BF16),
            pltpu.VMEM((64, 128), F32),
            pltpu.VMEM((16, 384), BF16),
            pltpu.VMEM((2, 16, 16, 384), BF16),
            pltpu.VMEM((192, 576), BF16),
            dma((8,)), dma, dma, dma, dma((16,)), dma((16,)), dma((16,)), dma((16,)),
            dma((4,)), dma((4,)), dma((16,)), dma((16,)), dma((16,)), dma((16,)),
        ],
        compiler_params=pltpu.CompilerParams(
            collective_id=0, has_side_effects=True, vmem_limit_bytes=32 * 2**20
        ),
    )(cholesky, active_coeff.T, pair_density.reshape(576, 576))


def solution(mesh):
    return jax.shard_map(
        shards,
        mesh=mesh,
        in_specs=(P("vec", "orb", None), P(), P()),
        out_specs=(P(("orb", "vec"), None, None), P(("orb", "vec"), None)),
        check_vma=False,
    )
```

time: 277 us -> 42.1 us (0.15)
  the two profiles are of different devices: /device:TPU:32 before, /device:TPU:1 now
where the time goes in v1:
time: 42.1 us; the launch traced here: 41.9 us
  Pallas kernels  35.7 us (85%)
  local copies, waits for them, and re-layouts  5.46 us (13%)
  between operations  0.65 us (2%)
    pallas_call x1, Pallas kernels, shards(): pl.pallas_call(kernel, name='half_active_fock', out_shape=(jax.ShapeDtype...  35.7 us
    unnamed x8, local copies, waits for them, and re-layouts  5.46 us

profile of v1, /device:TPU:1, one launch (start us, length us, event | category | flops | bytes accessed | tf_op | source)
XLA Modules:
  0.0 41.9 jit_solution(6699537504435813300)
XLA Ops:
  0.6 0.0 copy-start
  0.6 2.2 %copy-done = bf16[4,256,2048]{2,1,0:T(8,128)(2,1)S(1)} copy-done((bf16[4,256,2048]{2,1,0:T(8,128)(2,1)S(1)}, bf16[4,256,2048]{2,1,0:T(8,128)(2,1)}, u32[]{:S(2)}) %copy-start) | copy-done | bytes 4194328
  2.8 0.0 copy-start.1
  2.8 1.1 %copy-done.1 = bf16[24,24,576]{2,1,0:T(8,128)(2,1)S(1)} copy-done((bf16[24,24,576]{2,1,0:T(8,128)(2,1)S(1)}, bf16[24,24,576]{2,1,0:T(8,128)(2,1)}, u32[]{:S(2)}) %copy-start.1) | copy-done | bytes 663576
  3.9 0.0 copy-start.2
  3.9 0.9 %copy-done.2 = bf16[2048,24]{0,1:T(8,128)(2,1)S(1)} copy-done((bf16[2048,24]{0,1:T(8,128)(2,1)S(1)}, bf16[2048,24]{0,1:T(8,128)(2,1)}, u32[]{:S(2)}) %copy-start.2) | copy-done | bytes 98328
  4.8 35.7 %half_active_fock.1 = (f32[4,24,576]{2,1,0:T(8,128)S(1)}, f32[4,24]{1,0:T(4,128)S(1)}) custom-call(bf16[4,256,2048]{2,1,0:T(8,128)(2,1)S(1)} %copy-done, bf16[24,2048]{1,0:T(8,128)(2,1)S(1)} %bitcast.3, bf16[576,576]{1,0:T(8,128)(2,1)S(1)} %bitcast.2), custom_call_target="tpu_custom_call" | custom-call | tf_op jit(solution)/shard_map/half_active_fock/pallas_call | solution.py:239
  40.6 0.7 %copy.7 = f32[4,24,576]{2,1,0:T(8,128)} copy(f32[4,24,576]{2,1,0:T(8,128)S(1)} %get-tuple-element.4) | data formatting | bytes 442368
  41.3 0.6 %copy.8 = f32[4,24]{1,0:T(4,128)} copy(f32[4,24]{1,0:T(4,128)S(1)} %get-tuple-element.5) | data formatting | bytes 768
Async XLA Ops:
  0.6 2.2 %copy-start = (bf16[4,256,2048]{2,1,0:T(8,128)(2,1)S(1)}, bf16[4,256,2048]{2,1,0:T(8,128)(2,1)}, u32[]{:S(2)}) copy-start(bf16[4,256,2048]{2,1,0:T(8,128)(2,1)} %chol.1) | copy-start | bytes 12582916
  2.8 1.1 %copy-start.1 = (bf16[24,24,576]{2,1,0:T(8,128)(2,1)S(1)}, bf16[24,24,576]{2,1,0:T(8,128)(2,1)}, u32[]{:S(2)}) copy-start(bf16[24,24,576]{2,1,0:T(8,128)(2,1)} %param.5) | copy-start | bytes 1990660
  3.9 0.9 %copy-start.2 = (bf16[2048,24]{0,1:T(8,128)(2,1)S(1)}, bf16[2048,24]{0,1:T(8,128)(2,1)}, u32[]{:S(2)}) copy-start(bf16[2048,24]{0,1:T(8,128)(2,1)} %param.4) | copy-start | bytes 294916

commit v2 on v1

--- a/solution.py
+++ b/solution.py
@@ -13,10 +13,10 @@
 
 
 def kernel(
-    chol, coeff_t, density, out, fock,
-    chol_v, coeff_pad, coeff_blk, density_v, half32, spread, rows_out, rows_in, rows32,
-    turn_out, turn_in, turn32, part32, pair_in, part_out, part_in, sum32, block_out, gathered, ints,
-    chol_sem, density_sem, pair_send, pair_recv, rows_send, rows_recv, part_send, part_recv,
+    chol, coeff_h, density, out, fock,
+    chol_v, coeff_t, coeff_pad, coeff_blk, density_v, half32, rows_out, rows_in, rows32,
+    turn_out, turn_in, part32, pair_in, part_out, part_in, sum32, block_out, gathered, ints,
+    chol_sem, coeff_sem, density_sem, pair_send, pair_recv, rows_send, rows_recv, part_send, part_recv,
     turn_send, turn_recv, block_send, block_recv, share_send, share_recv,
 ):
     vec, orb = lax.axis_index("vec"), lax.axis_index("orb")
@@ -36,24 +36,27 @@
             src_ref=src, dst_ref=dst, send_sem=send, recv_sem=recv, device_id=device, device_id_type=MESH
         )
 
-    barrier = pltpu.get_barrier_semaphore()
-    pl.semaphore_signal(barrier, inc=1, device_id=sibling, device_id_type=MESH)
-
-    @pl.loop(1, 16)
-    def _(k):
-        pl.semaphore_signal(barrier, inc=1, device_id=column(k), device_id_type=MESH)
-        pl.semaphore_signal(barrier, inc=1, device_id=plane(k), device_id_type=MESH)
-
     def fetch(n):
         piece = (n // 2, pl.ds((n % 2) * 128, 128))
         return pltpu.make_async_copy(chol.at[piece], chol_v.at[piece], chol_sem.at[n])
 
+    coeff_copy = pltpu.make_async_copy(coeff_h, coeff_t, coeff_sem)
+    coeff_copy.start()
     for n in range(8):
         fetch(n).start()
     density_copy = pltpu.make_async_copy(density, density_v, density_sem)
     density_copy.start()
 
+    barrier = pltpu.get_barrier_semaphore()
+    pl.semaphore_signal(barrier, inc=1, device_id=sibling, device_id_type=MESH)
+
+    @pl.loop(1, 16)
+    def _(k):
+        pl.semaphore_signal(barrier, inc=1, device_id=column(k), device_id_type=MESH)
+        pl.semaphore_signal(barrier, inc=1, device_id=plane(k), device_id_type=MESH)
+
     coeff_pad[...] = jnp.zeros_like(coeff_pad)
+    coeff_copy.wait()
     coeff_pad[0:24, :] = coeff_t[...]
     for n in range(2):
         lanes = pl.ds(pl.multiple_of(orb * 256 + n * 128, 128), 128)
@@ -85,21 +88,26 @@
     pair_copy = remote(part32.at[1 - core], pair_in, pair_send, pair_recv, sibling)
     pair_copy.start()
 
-    for yy in range(4):
-        for zz in range(4):
-            at = zz * 16 + yy * 4
-            group = half32[pl.ds(at, 16, stride=64), :]
-            for i in range(1, 4):
-                group = group + pltpu.roll(half32[pl.ds(at + i, 16, stride=64), :], 24 * i, 1)
-            spread[yy * 64 + zz * 16 : yy * 64 + zz * 16 + 16, :] = group
-        for xx in range(4):
-            rows_out[xx * 4 + yy] = spread[pl.ds(yy * 64 + xx, 16, stride=4), :].astype(BF16)
+    lane = lax.broadcasted_iota(jnp.int32, (16, 128), 1)
+    for zz in range(4):
+        tiles = [None] * 3
+        for n in range(16):
+            at, shift = divmod(24 * n, 128)
+            group = half32[pl.ds(zz * 16 + n, 16, stride=64), :]
+            group = pltpu.roll(group, shift, 1) if shift else group
+            if shift > 104:
+                tiles[at + 1] = jnp.where(lane < shift, group, 0.0)
+                group = jnp.where(lane >= shift, group, 0.0)
+            tiles[at] = group if tiles[at] is None else tiles[at] + group
+        for n in range(3):
+            rows_out[zz, :, n * 128 : n * 128 + 128] = tiles[n].astype(BF16)
 
     def rows_copy(k):
-        to = ((x + k // 4) % 4) * 4 + (y + k % 4) % 4
-        return remote(rows_out.at[to], rows_in.at[k], rows_send.at[k], rows_recv.at[k], plane(k))
-
-    @pl.loop(1, 16)
+        to = (zh + k) % 4
+        device = (x * 16 + to * 4 + y, orb)
+        return remote(rows_out.at[to], rows_in.at[k], rows_send.at[k], rows_recv.at[k], device)
+
+    @pl.loop(1, 4)
     def _(k):
         rows_copy(k).start()
 
@@ -115,28 +123,35 @@
     def _(k):
         part_copy(k).start()
 
-    rows_in[0] = rows_out[x * 4 + y]
-
-    @pl.loop(1, 16)
+    rows_in[0] = rows_out[zh]
+
+    @pl.loop(1, 4)
     def _(k):
         rows_copy(k).wait_recv()
 
-    for k in range(16):
-        rows32[k * 16 : k * 16 + 16, :] = rows_in[k].astype(F32)
-    for zz in range(4):
-        for q in range(4):
-            turn_out[zz, q * 16 : q * 16 + 16, :] = rows32[pl.ds(zz * 4 + q, 16, stride=16), :].astype(BF16)
+    for k in range(4):
+        for n in range(3):
+            rows32[n * 64 + k * 16 : n * 64 + k * 16 + 16, :] = rows_in[k, :, n * 128 : n * 128 + 128].astype(F32)
+    for xx in range(4):
+        t = [rows32[pl.ds(n * 64 + xx, 16, stride=4), :] for n in range(3)]
+        owners = (
+            t[0],
+            jnp.where(lane < 32, pltpu.roll(t[0], 32, 1), pltpu.roll(t[1], 32, 1)),
+            jnp.where(lane < 64, pltpu.roll(t[1], 64, 1), pltpu.roll(t[2], 64, 1)),
+            pltpu.roll(t[2], 96, 1),
+        )
+        for yy in range(4):
+            turn_out[xx * 4 + yy] = owners[yy].astype(BF16)
 
     def turn_copy(k):
-        to = (zh + k) % 4
-        device = (x * 16 + to * 4 + y, orb)
-        return remote(turn_out.at[to], turn_in.at[k], turn_send.at[k], turn_recv.at[k], device)
-
-    @pl.loop(1, 4)
+        to = ((x + k // 4) % 4) * 4 + (y + k % 4) % 4
+        return remote(turn_out.at[to], turn_in.at[k], turn_send.at[k], turn_recv.at[k], plane(k))
+
+    @pl.loop(1, 16)
     def _(k):
         turn_copy(k).start()
 
-    turn_in[0] = turn_out[zh]
+    turn_in[0] = turn_out[x * 4 + y]
 
     @pl.loop(1, 16)
     def _(k):
@@ -148,7 +163,6 @@
             total = total + part_in[4 * h + n].astype(F32)
         sum32[h * 16 : h * 16 + 16, :] = total
     piece = [sum32[pl.ds(j, 16, stride=4), :] for j in range(4)]
-    lane = lax.broadcasted_iota(jnp.int32, (16, 128), 1)
     one, two, three = pltpu.roll(piece[1], 72, 1), pltpu.roll(piece[2], 16, 1), pltpu.roll(piece[3], 88, 1)
     left = (piece[0] + jnp.where(lane >= 72, one, 0.0)).astype(BF16)
     middle = (jnp.where(lane < 16, one, 0.0) + two + jnp.where(lane >= 88, three, 0.0)).astype(BF16)
@@ -170,15 +184,6 @@
 
     share_copy(0).start()
 
-    @pl.loop(1, 4)
-    def _(k):
-        turn_copy(k).wait_recv()
-
-    for k in range(4):
-        turn32[k * 64 : k * 64 + 64, :] = turn_in[k].astype(F32)
-    own = jnp.concatenate([turn32[pl.ds(k, 16, stride=16), :] for k in range(16)], axis=0)
-    own = own.astype(BF16)[:, 0:96]
-
     @pl.loop(1, 16)
     def _(k):
         block_copy(k).wait_recv()
@@ -189,6 +194,11 @@
         there = gathered.at[1 - core, k]
         remote(there, there, share_send.at[k], share_recv.at[k], sibling).wait_recv()
 
+    @pl.loop(1, 16)
+    def _(k):
+        turn_copy(k).wait_recv()
+
+    own = turn_in[...].reshape(256, 128)[:, 0:96]
     first = lax.dot_general(own, gathered[0].reshape(256, 384), TN, preferred_element_type=F32)
     second = lax.dot_general(own, gathered[1].reshape(256, 384), TN, preferred_element_type=F32)
     lane = lax.broadcasted_iota(jnp.int32, (96, 128), 1)
@@ -222,39 +232,38 @@
 
     @pl.loop(1, 16)
     def _(k):
-        rows_copy(k).wait_send()
+        turn_copy(k).wait_send()
         part_copy(k).wait_send()
         block_copy(k).wait_send()
         share_copy(k).wait_send()
 
     @pl.loop(1, 4)
     def _(k):
-        turn_copy(k).wait_send()
+        rows_copy(k).wait_send()
 
 
 def shards(cholesky, active_coeff, pair_density):
     vmem = pl.BlockSpec(memory_space=pltpu.VMEM)
-    hbm = pl.BlockSpec(memory_space=pl.ANY)
+    hbm = pl.BlockSpec(memory_space=pltpu.HBM)
     dma = pltpu.SemaphoreType.DMA
     return pl.pallas_call(
         kernel,
         name="half_active_fock",
         out_shape=(jax.ShapeDtypeStruct((4, 24, 576), F32), jax.ShapeDtypeStruct((4, 24), F32)),
-        in_specs=[hbm, vmem, hbm],
+        in_specs=[hbm, hbm, hbm],
         out_specs=(vmem, vmem),
         scratch_shapes=[
             pltpu.VMEM((4, 256, 2048), BF16),
+            pltpu.VMEM((24, 2048), BF16),
             pltpu.VMEM((128, 2048), BF16),
             pltpu.VMEM((48, 128), F32),
             pltpu.VMEM((576, 576), BF16),
             pltpu.VMEM((1024, 128), F32),
-            pltpu.VMEM((256, 128), F32),
+            pltpu.VMEM((4, 16, 384), BF16),
+            pltpu.VMEM((4, 16, 384), BF16),
+            pltpu.VMEM((192, 128), F32),
             pltpu.VMEM((16, 16, 128), BF16),
             pltpu.VMEM((16, 16, 128), BF16),
-            pltpu.VMEM((256, 128), F32),
-            pltpu.VMEM((4, 64, 128), BF16),
-            pltpu.VMEM((4, 64, 128), BF16),
-            pltpu.VMEM((256, 128), F32),
             pltpu.VMEM((2, 16, 128), F32),
             pltpu.VMEM((16, 128), F32),
             pltpu.VMEM((16, 128), BF16),
@@ -263,13 +272,18 @@
             pltpu.VMEM((16, 384), BF16),
             pltpu.VMEM((2, 16, 16, 384), BF16),
             pltpu.VMEM((192, 576), BF16),
-            dma((8,)), dma, dma, dma, dma((16,)), dma((16,)), dma((16,)), dma((16,)),
-            dma((4,)), dma((4,)), dma((16,)), dma((16,)), dma((16,)), dma((16,)),
+            dma((8,)), dma, dma, dma, dma, dma((4,)), dma((4,)), dma((16,)), dma((16,)),
+            dma((16,)), dma((16,)), dma((16,)), dma((16,)), dma((16,)), dma((16,)),
         ],
         compiler_params=pltpu.CompilerParams(
-            collective_id=0, has_side_effects=True, vmem_limit_bytes=32 * 2**20
+            collective_id=0, has_side_effects=True, vmem_limit_bytes=16 * 2**20
         ),
-    )(cholesky, active_coeff.T, pair_density.reshape(576, 576))
+    )(
+        *(
+            pltpu.with_memory_space_constraint(array, pltpu.HBM)
+            for array in (cholesky, active_coeff.T, pair_density.reshape(576, 576))
+        )
+    )
 
 
 def solution(mesh):

time: 42.1 us -> 41.3 us (0.981)
  local copies, waits for them, and re-layouts: 5.46 us -> 1.27 us
  Pallas kernels: 35.7 us -> 39.3 us
    unnamed x8 -> x2, local copies, waits for them, and re-layouts: 5.46 us -> 1.27 us
    pallas_call x1, Pallas kernels: 35.7 us -> 39.3 us  [shards(): pl.pallas_call(kernel, name='half_active_fock', out_shape=(jax.ShapeDtype...]
where the time goes in v2:
time: 41.3 us; the launch traced here: 41.2 us
  Pallas kernels  39.3 us (95%)
  local copies, waits for them, and re-layouts  1.27 us (3%)
  between operations  0.64 us (2%)
    pallas_call x1, Pallas kernels, shards(): pl.pallas_call(kernel, name='half_active_fock', out_shape=(jax.ShapeDtype...  39.3 us
    unnamed x2, local copies, waits for them, and re-layouts  1.27 us

profile of v2, /device:TPU:1, one launch (start us, length us, event | category | flops | bytes accessed | tf_op | source)
XLA Modules:
  0.0 41.2 jit_solution(12858749439693374621)
XLA Ops:
  0.6 39.3 %half_active_fock.1 = (f32[4,24,576]{2,1,0:T(8,128)S(1)}, f32[4,24]{1,0:T(4,128)S(1)}) custom-call(bf16[4,256,2048]{2,1,0:T(8,128)(2,1)} %chol.1, bf16[24,2048]{1,0:T(8,128)(2,1)} %bitcast.3, bf16[576,576]{1,0:T(8,128)(2,1)} %bitcast.2), custom_call_target="tpu_custom_call" | custom-call | tf_op jit(solution)/shard_map/half_active_fock/pallas_call | solution.py:249
  39.9 0.7 %copy.7 = f32[4,24,576]{2,1,0:T(8,128)} copy(f32[4,24,576]{2,1,0:T(8,128)S(1)} %get-tuple-element.4) | data formatting | bytes 442368
  40.6 0.6 %copy.8 = f32[4,24]{1,0:T(4,128)} copy(f32[4,24]{1,0:T(4,128)S(1)} %get-tuple-element.5) | data formatting | bytes 768

commit v3 on v2

--- a/solution.py
+++ b/solution.py
@@ -14,10 +14,10 @@
 
 def kernel(
     chol, coeff_h, density, out, fock,
-    chol_v, coeff_t, coeff_pad, coeff_blk, density_v, half32, rows_out, rows_in, rows32,
+    chol_v, coeff_t, coeff_blk, density_v, half32, rows_out, rows_in, rows32,
     turn_out, turn_in, part32, pair_in, part_out, part_in, sum32, block_out, gathered, ints,
     chol_sem, coeff_sem, density_sem, pair_send, pair_recv, rows_send, rows_recv, part_send, part_recv,
-    turn_send, turn_recv, block_send, block_recv, share_send, share_recv,
+    turn_send, turn_recv, block_send, block_recv,
 ):
     vec, orb = lax.axis_index("vec"), lax.axis_index("orb")
     x, zh, y = vec // 16, (vec // 4) % 4, vec % 4
@@ -27,9 +27,20 @@
         return (((x + k // 4) % 4) * 16 + zh * 4 + (y + k % 4) % 4, orb)
 
     def column(k):
-        return (x * 16 + ((zh + k // 4) % 4) * 4 + y, ((zl + k % 4) % 4) * 2 + core)
+        to = (zh * 4 + zl + k) % 16
+        return (x * 16 + (to // 4) * 4 + y, (to % 4) * 2 + core)
+
+    def column_to(z):
+        return (z - zh * 4 - zl + 16) % 16
+
+    def plane_to(n):
+        return ((n // 4 - x + 4) % 4) * 4 + (n % 4 - y + 4) % 4
 
     sibling = (vec, zl * 2 + 1 - core)
+
+    def chips(n):
+        vec_to, _ = plane(n // 2)
+        return (vec_to, zl * 2 + (core + n) % 2)
 
     def remote(src, dst, send, recv, device):
         return pltpu.make_async_remote_copy(
@@ -37,27 +48,34 @@
         )
 
     def fetch(n):
-        piece = (n // 2, pl.ds((n % 2) * 128, 128))
+        piece = (slice(None), slice(None), pl.ds(n * 512, 512))
         return pltpu.make_async_copy(chol.at[piece], chol_v.at[piece], chol_sem.at[n])
 
     coeff_copy = pltpu.make_async_copy(coeff_h, coeff_t, coeff_sem)
     coeff_copy.start()
-    for n in range(8):
+    for n in range(4):
         fetch(n).start()
     density_copy = pltpu.make_async_copy(density, density_v, density_sem)
-    density_copy.start()
 
     barrier = pltpu.get_barrier_semaphore()
+
     pl.semaphore_signal(barrier, inc=1, device_id=sibling, device_id_type=MESH)
 
-    @pl.loop(1, 16)
-    def _(k):
-        pl.semaphore_signal(barrier, inc=1, device_id=column(k), device_id_type=MESH)
-        pl.semaphore_signal(barrier, inc=1, device_id=plane(k), device_id_type=MESH)
-
-    coeff_pad[...] = jnp.zeros_like(coeff_pad)
+    @pl.loop(0, 16)
+    def _(n):
+        k = column_to(n)
+        p = plane_to(n)
+
+        @pl.when(k != 0)
+        def _():
+            pl.semaphore_signal(barrier, inc=1, device_id=column(k), device_id_type=MESH)
+
+        @pl.when(p != 0)
+        def _():
+            pl.semaphore_signal(barrier, inc=1, device_id=chips(2 * p + 1 - core), device_id_type=MESH)
+            pl.semaphore_signal(barrier, inc=1, device_id=chips(2 * p + core), device_id_type=MESH)
+
     coeff_copy.wait()
-    coeff_pad[0:24, :] = coeff_t[...]
     for n in range(2):
         lanes = pl.ds(pl.multiple_of(orb * 256 + n * 128, 128), 128)
         coeff_blk[n * 24 : n * 24 + 24, :] = coeff_t[:, lanes].astype(F32)
@@ -69,24 +87,39 @@
         axis=1,
     ).astype(BF16)
 
+    turned = None
+    half32[...] = jnp.zeros_like(half32)
+    for n in range(4):
+        fetch(n).wait()
+        term = lax.dot_general(
+            coeff_t[:, n * 512 : n * 512 + 512],
+            chol_v[:, :, n * 512 : n * 512 + 512].reshape(1024, 512),
+            NT,
+            preferred_element_type=F32,
+        )
+        turned = turned + term if n else term
+    density_copy.start()
+    turned = turned.astype(BF16)
+    stacked = jnp.concatenate([turned[:, q * 256 : q * 256 + 256] for q in range(4)], axis=0)
+    part = lax.dot_general(coeff_rows, stacked, NT, preferred_element_type=F32)
+    part = jnp.concatenate([part, jnp.zeros((24, 32), F32)], axis=1)
+    lane8 = lax.broadcasted_iota(jnp.int32, (8, 128), 1)
     for q in range(4):
-        for n in range(2):
-            fetch(2 * q + n).wait()
-            rows = lax.dot_general(
-                chol_v[q, n * 128 : n * 128 + 128, :], coeff_pad[...], NT, preferred_element_type=F32
-            )
-            half32[q * 256 + n * 128 : q * 256 + n * 128 + 128, :] = rows.astype(BF16).astype(F32)
-        part = jnp.dot(
-            coeff_rows, half32[q * 256 : q * 256 + 256, :].astype(BF16), preferred_element_type=F32
-        )
-        packed = part[0:8] + pltpu.roll(part[8:16], 24, 1) + pltpu.roll(part[16:24], 48, 1)
+        packed = jnp.zeros((8, 128), F32)
+        for k in range(3):
+            piece = part[k * 8 : k * 8 + 8]
+            shift = (24 * (k - q)) % 128
+            piece = pltpu.roll(piece, shift, 1) if shift else piece
+            packed = jnp.where((lane8 >= 24 * k) & (lane8 < 24 * k + 24), piece, packed)
         part32[0, q * 4 : q * 4 + 4, :] = packed[0:4]
         part32[1, q * 4 : q * 4 + 4, :] = packed[4:8]
 
-    pl.semaphore_wait(barrier, 31)
+    pl.semaphore_wait(barrier, 46)
 
     pair_copy = remote(part32.at[1 - core], pair_in, pair_send, pair_recv, sibling)
     pair_copy.start()
+
+    half32[:, 0:24] = turned.astype(F32).T
 
     lane = lax.broadcasted_iota(jnp.int32, (16, 128), 1)
     for zz in range(4):
@@ -119,9 +152,13 @@
     def part_copy(k):
         return remote(part_out, part_in.at[k], part_send.at[k], part_recv.at[k], column(k))
 
-    @pl.loop(1, 16)
-    def _(k):
-        part_copy(k).start()
+    @pl.loop(0, 16)
+    def _(n):
+        k = column_to(n)
+
+        @pl.when(k != 0)
+        def _():
+            part_copy(k).start()
 
     rows_in[0] = rows_out[zh]
 
@@ -147,20 +184,24 @@
         to = ((x + k // 4) % 4) * 4 + (y + k % 4) % 4
         return remote(turn_out.at[to], turn_in.at[k], turn_send.at[k], turn_recv.at[k], plane(k))
 
+    @pl.loop(0, 16)
+    def _(n):
+        k = plane_to(n)
+
+        @pl.when(k != 0)
+        def _():
+            turn_copy(k).start()
+
+    turn_in[0] = turn_out[x * 4 + y]
+
     @pl.loop(1, 16)
     def _(k):
-        turn_copy(k).start()
-
-    turn_in[0] = turn_out[x * 4 + y]
-
-    @pl.loop(1, 16)
-    def _(k):
         part_copy(k).wait_recv()
 
     for h in range(4):
-        total = part_in[4 * h].astype(F32)
+        total = part_in[(4 * h + zl) % 16].astype(F32)
         for n in range(1, 4):
-            total = total + part_in[4 * h + n].astype(F32)
+            total = total + part_in[(4 * h + zl - n + 16) % 16].astype(F32)
         sum32[h * 16 : h * 16 + 16, :] = total
     piece = [sum32[pl.ds(j, 16, stride=4), :] for j in range(4)]
     one, two, three = pltpu.roll(piece[1], 72, 1), pltpu.roll(piece[2], 16, 1), pltpu.roll(piece[3], 88, 1)
@@ -171,28 +212,27 @@
         block_out[:, n * 128 : n * 128 + 128] = tile
         gathered[core, 0, :, n * 128 : n * 128 + 128] = tile
 
-    def block_copy(k):
-        return remote(block_out, gathered.at[core, k], block_send.at[k], block_recv.at[k], plane(k))
-
-    def share_copy(k):
-        there = gathered.at[core, k]
-        return remote(there, there, share_send.at[k], share_recv.at[k], sibling)
+    def block_copy(n, source):
+        there = gathered.at[source, n // 2]
+        return remote(block_out, there, block_send.at[n], block_recv.at[source, n // 2], chips(n))
+
+    block_copy(1, core).start()
+
+    @pl.loop(0, 16)
+    def _(n):
+        k = plane_to(n)
+
+        @pl.when(k != 0)
+        def _():
+            block_copy(2 * k + 1 - core, core).start()
+            block_copy(2 * k + core, core).start()
 
     @pl.loop(1, 16)
     def _(k):
-        block_copy(k).start()
-
-    share_copy(0).start()
-
-    @pl.loop(1, 16)
-    def _(k):
-        block_copy(k).wait_recv()
-        share_copy(k).start()
-
-    @pl.loop(0, 16)
-    def _(k):
-        there = gathered.at[1 - core, k]
-        remote(there, there, share_send.at[k], share_recv.at[k], sibling).wait_recv()
+        block_copy(2 * k, core).wait_recv()
+        block_copy(2 * k, 1 - core).wait_recv()
+
+    block_copy(1, 1 - core).wait_recv()
 
     @pl.loop(1, 16)
     def _(k):
@@ -228,14 +268,14 @@
     fock[...] = jnp.dot(kept, pick.astype(F32), precision=lax.Precision.HIGHEST, preferred_element_type=F32)
 
     pair_copy.wait_send()
-    share_copy(0).wait_send()
+    block_copy(1, core).wait_send()
 
     @pl.loop(1, 16)
     def _(k):
         turn_copy(k).wait_send()
         part_copy(k).wait_send()
-        block_copy(k).wait_send()
-        share_copy(k).wait_send()
+        block_copy(2 * k, core).wait_send()
+        block_copy(2 * k + 1, core).wait_send()
 
     @pl.loop(1, 4)
     def _(k):
@@ -255,7 +295,6 @@
         scratch_shapes=[
             pltpu.VMEM((4, 256, 2048), BF16),
             pltpu.VMEM((24, 2048), BF16),
-            pltpu.VMEM((128, 2048), BF16),
             pltpu.VMEM((48, 128), F32),
             pltpu.VMEM((576, 576), BF16),
             pltpu.VMEM((1024, 128), F32),
@@ -272,8 +311,8 @@
             pltpu.VMEM((16, 384), BF16),
             pltpu.VMEM((2, 16, 16, 384), BF16),
             pltpu.VMEM((192, 576), BF16),
-            dma((8,)), dma, dma, dma, dma, dma((4,)), dma((4,)), dma((16,)), dma((16,)),
-            dma((16,)), dma((16,)), dma((16,)), dma((16,)), dma((16,)), dma((16,)),
+            dma((4,)), dma, dma, dma, dma, dma((4,)), dma((4,)), dma((16,)), dma((16,)),
+            dma((16,)), dma((16,)), dma((32,)), dma((2, 16)),
         ],
         compiler_params=pltpu.CompilerParams(
             collective_id=0, has_side_effects=True, vmem_limit_bytes=16 * 2**20

time: 41.3 us -> 37.6 us (0.910)
  Pallas kernels: 39.3 us -> 35.5 us
    pallas_call x1, Pallas kernels: 39.3 us -> 35.5 us  [shards(): pl.pallas_call(kernel, name='half_active_fock', out_shape=(jax.ShapeDtype...]
where the time goes in v3:
time: 37.6 us; the launch traced here: 37.4 us
  Pallas kernels  35.5 us (94%)
  local copies, waits for them, and re-layouts  1.27 us (3%)
  between operations  0.64 us (2%)
    pallas_call x1, Pallas kernels, shards(): pl.pallas_call(kernel, name='half_active_fock', out_shape=(jax.ShapeDtype...  35.5 us
    unnamed x2, local copies, waits for them, and re-layouts  1.27 us

profile of v3, /device:TPU:1, one launch (start us, length us, event | category | flops | bytes accessed | tf_op | source)
XLA Modules:
  0.0 37.4 jit_solution(9373344698555804881)
XLA Ops:
  0.6 35.5 %half_active_fock.1 = (f32[4,24,576]{2,1,0:T(8,128)S(1)}, f32[4,24]{1,0:T(4,128)S(1)}) custom-call(bf16[4,256,2048]{2,1,0:T(8,128)(2,1)} %chol.1, bf16[24,2048]{1,0:T(8,128)(2,1)} %bitcast.3, bf16[576,576]{1,0:T(8,128)(2,1)} %bitcast.2), custom_call_target="tpu_custom_call" | custom-call | tf_op jit(solution)/shard_map/half_active_fock/pallas_call | solution.py:289
  36.2 0.7 %copy.7 = f32[4,24,576]{2,1,0:T(8,128)} copy(f32[4,24,576]{2,1,0:T(8,128)S(1)} %get-tuple-element.4) | data formatting | bytes 442368
  36.9 0.6 %copy.8 = f32[4,24]{1,0:T(4,128)} copy(f32[4,24]{1,0:T(4,128)S(1)} %get-tuple-element.5) | data formatting | bytes 768

commit v4 on v3

--- a/solution.py
+++ b/solution.py
@@ -11,12 +11,14 @@
 NT = (((1,), (1,)), ((), ()))
 TN = (((0,), (0,)), ((), ()))
 
+CUTS = (0, 512, 1024, 1536, 1792, 2048)
+
 
 def kernel(
-    chol, coeff_h, density, out, fock,
-    chol_v, coeff_t, coeff_blk, density_v, half32, rows_out, rows_in, rows32,
-    turn_out, turn_in, part32, pair_in, part_out, part_in, sum32, block_out, gathered, ints,
-    chol_sem, coeff_sem, density_sem, pair_send, pair_recv, rows_send, rows_recv, part_send, part_recv,
+    chol, coeff_h, out,
+    chol_v, coeff_t, coeff_blk, half32, rows_out, rows_in, rows32,
+    turn_out, turn_in, part32, pair_in, part_out, part_in, sum32, block_out, gathered,
+    chol_sem, coeff_sem, pair_send, pair_recv, rows_send, rows_recv, part_send, part_recv,
     turn_send, turn_recv, block_send, block_recv,
 ):
     vec, orb = lax.axis_index("vec"), lax.axis_index("orb")
@@ -42,38 +44,44 @@
         vec_to, _ = plane(n // 2)
         return (vec_to, zl * 2 + (core + n) % 2)
 
+    def quad(n):
+        return (vec, ((zl // 2) * 2 + (zl + n // 2) % 2) * 2 + (core + n) % 2)
+
     def remote(src, dst, send, recv, device):
         return pltpu.make_async_remote_copy(
             src_ref=src, dst_ref=dst, send_sem=send, recv_sem=recv, device_id=device, device_id_type=MESH
         )
 
     def fetch(n):
-        piece = (slice(None), slice(None), pl.ds(n * 512, 512))
+        piece = (slice(None), slice(None), pl.ds(CUTS[n], CUTS[n + 1] - CUTS[n]))
         return pltpu.make_async_copy(chol.at[piece], chol_v.at[piece], chol_sem.at[n])
 
     coeff_copy = pltpu.make_async_copy(coeff_h, coeff_t, coeff_sem)
     coeff_copy.start()
-    for n in range(4):
+    for n in range(len(CUTS) - 1):
         fetch(n).start()
-    density_copy = pltpu.make_async_copy(density, density_v, density_sem)
 
     barrier = pltpu.get_barrier_semaphore()
-
-    pl.semaphore_signal(barrier, inc=1, device_id=sibling, device_id_type=MESH)
 
     @pl.loop(0, 16)
     def _(n):
         k = column_to(n)
-        p = plane_to(n)
 
         @pl.when(k != 0)
         def _():
             pl.semaphore_signal(barrier, inc=1, device_id=column(k), device_id_type=MESH)
 
-        @pl.when(p != 0)
+    pl.semaphore_signal(barrier, inc=1, device_id=sibling, device_id_type=MESH)
+    pl.semaphore_signal(barrier, inc=1, device_id=quad(3), device_id_type=MESH)
+
+    @pl.loop(0, 16)
+    def _(n):
+        k = plane_to(n)
+
+        @pl.when(k != 0)
         def _():
-            pl.semaphore_signal(barrier, inc=1, device_id=chips(2 * p + 1 - core), device_id_type=MESH)
-            pl.semaphore_signal(barrier, inc=1, device_id=chips(2 * p + core), device_id_type=MESH)
+            pl.semaphore_signal(barrier, inc=1, device_id=chips(2 * k + 1 - core), device_id_type=MESH)
+            pl.semaphore_signal(barrier, inc=1, device_id=chips(2 * k + core), device_id_type=MESH)
 
     coeff_copy.wait()
     for n in range(2):
@@ -89,16 +97,16 @@
 
     turned = None
     half32[...] = jnp.zeros_like(half32)
-    for n in range(4):
+    for n in range(len(CUTS) - 1):
         fetch(n).wait()
+        columns = slice(CUTS[n], CUTS[n + 1])
         term = lax.dot_general(
-            coeff_t[:, n * 512 : n * 512 + 512],
-            chol_v[:, :, n * 512 : n * 512 + 512].reshape(1024, 512),
+            coeff_t[:, columns],
+            chol_v[:, :, columns].reshape(1024, -1),
             NT,
             preferred_element_type=F32,
         )
         turned = turned + term if n else term
-    density_copy.start()
     turned = turned.astype(BF16)
     stacked = jnp.concatenate([turned[:, q * 256 : q * 256 + 256] for q in range(4)], axis=0)
     part = lax.dot_general(coeff_rows, stacked, NT, preferred_element_type=F32)
@@ -111,13 +119,18 @@
             shift = (24 * (k - q)) % 128
             piece = pltpu.roll(piece, shift, 1) if shift else piece
             packed = jnp.where((lane8 >= 24 * k) & (lane8 < 24 * k + 24), piece, packed)
-        part32[0, q * 4 : q * 4 + 4, :] = packed[0:4]
-        part32[1, q * 4 : q * 4 + 4, :] = packed[4:8]
-
-    pl.semaphore_wait(barrier, 46)
-
-    pair_copy = remote(part32.at[1 - core], pair_in, pair_send, pair_recv, sibling)
-    pair_copy.start()
+        at = (q % 2) * 4
+        part32[0, q // 2, at : at + 4, :] = packed[0:4]
+        part32[1, q // 2, at : at + 4, :] = packed[4:8]
+
+    pl.semaphore_wait(barrier, 47)
+
+    def pair_copy(n):
+        share = part32.at[(core + n) % 2, (zl + n // 2) % 2]
+        return remote(share, pair_in.at[n], pair_send.at[n], pair_recv.at[n], quad(n))
+
+    for n in (3, 2, 1):
+        pair_copy(n).start()
 
     half32[:, 0:24] = turned.astype(F32).T
 
@@ -144,8 +157,9 @@
     def _(k):
         rows_copy(k).start()
 
-    pair_copy.wait_recv()
-    mine = (part32[core] + pair_in[...]).astype(BF16)
+    for n in (1, 2, 3):
+        pair_copy(n).wait_recv()
+    mine = (part32[core, zl % 2] + pair_in[1] + pair_in[2] + pair_in[3]).astype(BF16)
     part_out[...] = mine
     part_in[0] = mine
 
@@ -184,14 +198,6 @@
         to = ((x + k // 4) % 4) * 4 + (y + k % 4) % 4
         return remote(turn_out.at[to], turn_in.at[k], turn_send.at[k], turn_recv.at[k], plane(k))
 
-    @pl.loop(0, 16)
-    def _(n):
-        k = plane_to(n)
-
-        @pl.when(k != 0)
-        def _():
-            turn_copy(k).start()
-
     turn_in[0] = turn_out[x * 4 + y]
 
     @pl.loop(1, 16)
@@ -199,10 +205,9 @@
         part_copy(k).wait_recv()
 
     for h in range(4):
-        total = part_in[(4 * h + zl) % 16].astype(F32)
-        for n in range(1, 4):
-            total = total + part_in[(4 * h + zl - n + 16) % 16].astype(F32)
-        sum32[h * 16 : h * 16 + 16, :] = total
+        for p in range(2):
+            total = part_in[(4 * h + zl - p + 16) % 16].astype(F32) + part_in[(4 * h + zl - p + 14) % 16].astype(F32)
+            sum32[h * 16 + p * 8 : h * 16 + p * 8 + 8, :] = total
     piece = [sum32[pl.ds(j, 16, stride=4), :] for j in range(4)]
     one, two, three = pltpu.roll(piece[1], 72, 1), pltpu.roll(piece[2], 16, 1), pltpu.roll(piece[3], 88, 1)
     left = (piece[0] + jnp.where(lane >= 72, one, 0.0)).astype(BF16)
@@ -226,6 +231,7 @@
         def _():
             block_copy(2 * k + 1 - core, core).start()
             block_copy(2 * k + core, core).start()
+            turn_copy(k).start()
 
     @pl.loop(1, 16)
     def _(k):
@@ -254,75 +260,84 @@
         width = min(128, 576 - n * 128)
         tile = tile[:, 0:width]
         out[:, :, n * 128 : n * 128 + width] = tile.reshape(4, 24, width)
-        high = tile.astype(BF16)
-        ints[0:96, n * 128 : n * 128 + width] = high
-        ints[96:192, n * 128 : n * 128 + width] = (tile - high.astype(F32)).astype(BF16)
-
-    density_copy.wait()
-    pairs = lax.dot_general(ints[...], density_v[...], NT, preferred_element_type=F32)
+
+    for n in (1, 2, 3):
+        pair_copy(n).wait_send()
+    block_copy(1, core).wait_send()
+
+    @pl.loop(1, 16)
+    def _(k):
+        turn_copy(k).wait_send()
+        part_copy(k).wait_send()
+        block_copy(2 * k, core).wait_send()
+        block_copy(2 * k + 1, core).wait_send()
+
+    @pl.loop(1, 4)
+    def _(k):
+        rows_copy(k).wait_send()
+
+
+def fock_kernel(ints, density, out, fock, split, out_sem):
+    copy = pltpu.make_async_copy(ints, out, out_sem)
+    copy.start()
+    tile = ints[...].reshape(96, 576)
+    high = tile.astype(BF16)
+    split[0:96, :] = high
+    split[96:192, :] = (tile - high.astype(F32)).astype(BF16)
+
+    pairs = lax.dot_general(split[...], density[...], NT, preferred_element_type=F32)
     pairs = pairs[0:96] + pairs[96:192]
     row = lax.broadcasted_iota(jnp.int32, (96, 576), 0) % 24
     col = lax.broadcasted_iota(jnp.int32, (96, 576), 1) % 24
     kept = jnp.where(row == col, pairs, 0.0).reshape(4, 24, 576).sum(axis=1)
     pick = lax.broadcasted_iota(jnp.int32, (576, 24), 0) // 24 == lax.broadcasted_iota(jnp.int32, (576, 24), 1)
     fock[...] = jnp.dot(kept, pick.astype(F32), precision=lax.Precision.HIGHEST, preferred_element_type=F32)
-
-    pair_copy.wait_send()
-    block_copy(1, core).wait_send()
-
-    @pl.loop(1, 16)
-    def _(k):
-        turn_copy(k).wait_send()
-        part_copy(k).wait_send()
-        block_copy(2 * k, core).wait_send()
-        block_copy(2 * k + 1, core).wait_send()
-
-    @pl.loop(1, 4)
-    def _(k):
-        rows_copy(k).wait_send()
+    copy.wait()
 
 
 def shards(cholesky, active_coeff, pair_density):
     vmem = pl.BlockSpec(memory_space=pltpu.VMEM)
     hbm = pl.BlockSpec(memory_space=pltpu.HBM)
     dma = pltpu.SemaphoreType.DMA
-    return pl.pallas_call(
+    ints = pl.pallas_call(
         kernel,
         name="half_active_fock",
-        out_shape=(jax.ShapeDtypeStruct((4, 24, 576), F32), jax.ShapeDtypeStruct((4, 24), F32)),
-        in_specs=[hbm, hbm, hbm],
-        out_specs=(vmem, vmem),
+        out_shape=jax.ShapeDtypeStruct((4, 24, 576), F32),
+        in_specs=[hbm, hbm],
+        out_specs=vmem,
         scratch_shapes=[
             pltpu.VMEM((4, 256, 2048), BF16),
             pltpu.VMEM((24, 2048), BF16),
             pltpu.VMEM((48, 128), F32),
-            pltpu.VMEM((576, 576), BF16),
             pltpu.VMEM((1024, 128), F32),
             pltpu.VMEM((4, 16, 384), BF16),
             pltpu.VMEM((4, 16, 384), BF16),
             pltpu.VMEM((192, 128), F32),
             pltpu.VMEM((16, 16, 128), BF16),
             pltpu.VMEM((16, 16, 128), BF16),
-            pltpu.VMEM((2, 16, 128), F32),
-            pltpu.VMEM((16, 128), F32),
-            pltpu.VMEM((16, 128), BF16),
-            pltpu.VMEM((16, 16, 128), BF16),
+            pltpu.VMEM((2, 2, 8, 128), F32),
+            pltpu.VMEM((4, 8, 128), F32),
+            pltpu.VMEM((8, 128), BF16),
+            pltpu.VMEM((16, 8, 128), BF16),
             pltpu.VMEM((64, 128), F32),
             pltpu.VMEM((16, 384), BF16),
             pltpu.VMEM((2, 16, 16, 384), BF16),
-            pltpu.VMEM((192, 576), BF16),
-            dma((4,)), dma, dma, dma, dma, dma((4,)), dma((4,)), dma((16,)), dma((16,)),
+            dma((len(CUTS) - 1,)), dma, dma((4,)), dma((4,)), dma((4,)), dma((4,)), dma((16,)), dma((16,)),
             dma((16,)), dma((16,)), dma((32,)), dma((2, 16)),
         ],
         compiler_params=pltpu.CompilerParams(
             collective_id=0, has_side_effects=True, vmem_limit_bytes=16 * 2**20
         ),
-    )(
-        *(
-            pltpu.with_memory_space_constraint(array, pltpu.HBM)
-            for array in (cholesky, active_coeff.T, pair_density.reshape(576, 576))
-        )
-    )
+    )(*(pltpu.with_memory_space_constraint(array, pltpu.HBM) for array in (cholesky, active_coeff.T)))
+    return pl.pallas_call(
+        fock_kernel,
+        name="fock",
+        out_shape=(jax.ShapeDtypeStruct((4, 24, 576), F32), jax.ShapeDtypeStruct((4, 24), F32)),
+        in_specs=[vmem, vmem],
+        out_specs=(hbm, vmem),
+        scratch_shapes=[pltpu.VMEM((192, 576), BF16), dma],
+        compiler_params=pltpu.CompilerParams(vmem_limit_bytes=16 * 2**20),
+    )(ints, pair_density.reshape(576, 576))
 
 
 def solution(mesh):

time: 37.6 us -> 36.6 us (0.973)
  local copies, waits for them, and re-layouts: 1.27 us -> 0.01 us
    unnamed x2, local copies, waits for them, and re-layouts: 1.27 us -> 0.01 us
    pallas_call x1 -> x2, Pallas kernels: 35.5 us -> 35.8 us  [the longest x1 34.4 us: shards(): pl.pallas_call(kernel, name='half_active_fock', out_shape=jax.ShapeDtypeS...]
where the time goes in v4:
time: 36.6 us; the launch traced here: 36.4 us
  Pallas kernels  35.8 us (98%)
  between operations  0.65 us (2%)
    pallas_call x1, Pallas kernels, shards(): pl.pallas_call(kernel, name='half_active_fock', out_shape=jax.ShapeDtypeS...  34.4 us
    pallas_call x1, Pallas kernels, shards(): pl.pallas_call(fock_kernel, name='fock', out_shape=(jax.ShapeDtypeStruct(...  1.34 us

profile of v4, /device:TPU:1, one launch (start us, length us, event | category | flops | bytes accessed | tf_op | source)
XLA Modules:
  0.0 36.4 jit_solution(433839105725862089)
XLA Ops:
  0.6 0.0 copy-start
  0.6 34.4 %half_active_fock.1.ints = f32[4,24,576]{2,1,0:T(8,128)S(1)} custom-call(bf16[4,256,2048]{2,1,0:T(8,128)(2,1)} %chol.1, bf16[24,2048]{1,0:T(8,128)(2,1)} %bitcast.3), custom_call_target="tpu_custom_call" | custom-call | tf_op jit(solution)/shard_map/half_active_fock/pallas_call | solution.py:302
  35.1 0.0 copy-done
  35.1 1.3 %fock.1 = (f32[4,24,576]{2,1,0:T(8,128)}, f32[4,24]{1,0:T(4,128)}) custom-call(f32[4,24,576]{2,1,0:T(8,128)S(1)} %half_active_fock.1.ints, bf16[576,576]{1,0:T(8,128)(2,1)S(1)} %bitcast.2), custom_call_target="tpu_custom_call" | custom-call | tf_op jit(solution)/shard_map/fock/pallas_call | solution.py:332
Async XLA Ops:
  0.6 34.5 %copy-start = (bf16[24,24,576]{2,1,0:T(8,128)(2,1)S(1)}, bf16[24,24,576]{2,1,0:T(8,128)(2,1)}, u32[]{:S(2)}) copy-start(bf16[24,24,576]{2,1,0:T(8,128)(2,1)} %param.5) | copy-start | bytes 1990660

commit v5 on v4

--- a/solution.py
+++ b/solution.py
@@ -19,7 +19,7 @@
     chol_v, coeff_t, coeff_blk, half32, rows_out, rows_in, rows32,
     turn_out, turn_in, part32, pair_in, part_out, part_in, sum32, block_out, gathered,
     chol_sem, coeff_sem, pair_send, pair_recv, rows_send, rows_recv, part_send, part_recv,
-    turn_send, turn_recv, block_send, block_recv,
+    turn_send, turn_recv, block_send, block_recv, share_send, share_recv,
 ):
     vec, orb = lax.axis_index("vec"), lax.axis_index("orb")
     x, zh, y = vec // 16, (vec // 4) % 4, vec % 4
@@ -198,6 +198,14 @@
         to = ((x + k // 4) % 4) * 4 + (y + k % 4) % 4
         return remote(turn_out.at[to], turn_in.at[k], turn_send.at[k], turn_recv.at[k], plane(k))
 
+    @pl.loop(0, 16)
+    def _(n):
+        k = plane_to(n)
+
+        @pl.when(k != 0)
+        def _():
+            turn_copy(k).start()
+
     turn_in[0] = turn_out[x * 4 + y]
 
     @pl.loop(1, 16)
@@ -217,28 +225,67 @@
         block_out[:, n * 128 : n * 128 + 128] = tile
         gathered[core, 0, :, n * 128 : n * 128 + 128] = tile
 
+    origin = vec // 16 + vec % 4 == 0
+
     def block_copy(n, source):
         there = gathered.at[source, n // 2]
         return remote(block_out, there, block_send.at[n], block_recv.at[source, n // 2], chips(n))
 
-    block_copy(1, core).start()
-
-    @pl.loop(0, 16)
+    def share_copy(n, source):
+        there = gathered.at[source, pl.ds(n * 8, 8)]
+        return remote(there, there, share_send.at[n], share_recv.at[n], sibling)
+
+    first_k = plane_to(0)
+
+    @pl.when(first_k != 0)
+    def _():
+        block_copy(2 * first_k + 1 - core, core).start()
+        block_copy(2 * first_k + core, core).start()
+
+    @pl.when(first_k == 0)
+    def _():
+        block_copy(1, core).start()
+
+    @pl.loop(1, 16)
     def _(n):
         k = plane_to(n)
 
         @pl.when(k != 0)
         def _():
-            block_copy(2 * k + 1 - core, core).start()
-            block_copy(2 * k + core, core).start()
-            turn_copy(k).start()
-
-    @pl.loop(1, 16)
-    def _(k):
-        block_copy(2 * k, core).wait_recv()
-        block_copy(2 * k, 1 - core).wait_recv()
-
-    block_copy(1, 1 - core).wait_recv()
+            block_copy(2 * k, core).start()
+
+    @pl.loop(1, 16)
+    def _(k):
+        part_copy(k).wait_send()
+
+    @pl.loop(1, 4)
+    def _(k):
+        rows_copy(k).wait_send()
+
+    for n in (1, 2, 3):
+        pair_copy(n).wait_send()
+
+    @pl.when(origin)
+    def _():
+        @pl.loop(1, 16)
+        def _(k):
+            block_copy(2 * k, core).wait_recv()
+            block_copy(2 * k, 1 - core).wait_recv()
+
+        block_copy(1, 1 - core).wait_recv()
+
+    @pl.when(jnp.logical_not(origin))
+    def _():
+        for n in range(2):
+
+            @pl.loop(n * 8 + 1 - n, n * 8 + 8)
+            def _(k):
+                block_copy(2 * k, core).wait_recv()
+
+            share_copy(n, core).start()
+
+        for n in range(2):
+            share_copy(n, 1 - core).wait_recv()
 
     @pl.loop(1, 16)
     def _(k):
@@ -261,20 +308,21 @@
         tile = tile[:, 0:width]
         out[:, :, n * 128 : n * 128 + width] = tile.reshape(4, 24, width)
 
-    for n in (1, 2, 3):
-        pair_copy(n).wait_send()
-    block_copy(1, core).wait_send()
+    @pl.when(origin)
+    def _():
+        block_copy(1, core).wait_send()
+
+    @pl.when(jnp.logical_not(origin))
+    def _():
+        block_copy(2 * first_k + 1, core).wait_send()
+        for n in range(2):
+            share_copy(n, core).wait_send()
+
 
     @pl.loop(1, 16)
     def _(k):
         turn_copy(k).wait_send()
-        part_copy(k).wait_send()
         block_copy(2 * k, core).wait_send()
-        block_copy(2 * k + 1, core).wait_send()
-
-    @pl.loop(1, 4)
-    def _(k):
-        rows_copy(k).wait_send()
 
 
 def fock_kernel(ints, density, out, fock, split, out_sem):
@@ -323,7 +371,7 @@
             pltpu.VMEM((16, 384), BF16),
             pltpu.VMEM((2, 16, 16, 384), BF16),
             dma((len(CUTS) - 1,)), dma, dma((4,)), dma((4,)), dma((4,)), dma((4,)), dma((16,)), dma((16,)),
-            dma((16,)), dma((16,)), dma((32,)), dma((2, 16)),
+            dma((16,)), dma((16,)), dma((32,)), dma((2, 16)), dma((2,)), dma((2,)),
         ],
         compiler_params=pltpu.CompilerParams(
             collective_id=0, has_side_effects=True, vmem_limit_bytes=16 * 2**20

time: 36.6 us -> 36 us (0.984)
  Pallas kernels: 35.8 us -> 35.2 us
    pallas_call x1, Pallas kernels: 34.4 us -> 33.9 us  [shards(): pl.pallas_call(kernel, name='half_active_fock', out_shape=jax.ShapeDtypeS...]
where the time goes in v5:
time: 36 us; the launch traced here: 35.9 us
  Pallas kernels  35.2 us (98%)
  between operations  0.65 us (2%)
    pallas_call x1, Pallas kernels, shards(): pl.pallas_call(kernel, name='half_active_fock', out_shape=jax.ShapeDtypeS...  33.9 us
    pallas_call x1, Pallas kernels, shards(): pl.pallas_call(fock_kernel, name='fock', out_shape=(jax.ShapeDtypeStruct(...  1.34 us

profile of v5, /device:TPU:1, one launch (start us, length us, event | category | flops | bytes accessed | tf_op | source)
XLA Modules:
  0.0 35.9 jit_solution(4584451571638892768)
XLA Ops:
  0.6 0.0 copy-start
  0.6 33.9 %half_active_fock.1.ints = f32[4,24,576]{2,1,0:T(8,128)S(1)} custom-call(bf16[4,256,2048]{2,1,0:T(8,128)(2,1)} %chol.1, bf16[24,2048]{1,0:T(8,128)(2,1)} %bitcast.3), custom_call_target="tpu_custom_call" | custom-call | tf_op jit(solution)/shard_map/half_active_fock/pallas_call | solution.py:350
  34.5 0.0 copy-done
  34.5 1.3 %fock.1 = (f32[4,24,576]{2,1,0:T(8,128)}, f32[4,24]{1,0:T(4,128)}) custom-call(f32[4,24,576]{2,1,0:T(8,128)S(1)} %half_active_fock.1.ints, bf16[576,576]{1,0:T(8,128)(2,1)S(1)} %bitcast.2), custom_call_target="tpu_custom_call" | custom-call | tf_op jit(solution)/shard_map/fock/pallas_call | solution.py:380
Async XLA Ops:
  0.6 33.9 %copy-start = (bf16[24,24,576]{2,1,0:T(8,128)(2,1)S(1)}, bf16[24,24,576]{2,1,0:T(8,128)(2,1)}, u32[]{:S(2)}) copy-start(bf16[24,24,576]{2,1,0:T(8,128)(2,1)} %param.5) | copy-start | bytes 1990660

commit v6 on v5

--- a/solution.py
+++ b/solution.py
@@ -9,7 +9,6 @@
 F32 = jnp.float32
 BF16 = jnp.bfloat16
 NT = (((1,), (1,)), ((), ()))
-TN = (((0,), (0,)), ((), ()))
 
 CUTS = (0, 512, 1024, 1536, 1792, 2048)
 
@@ -123,15 +122,6 @@
         part32[0, q // 2, at : at + 4, :] = packed[0:4]
         part32[1, q // 2, at : at + 4, :] = packed[4:8]
 
-    pl.semaphore_wait(barrier, 47)
-
-    def pair_copy(n):
-        share = part32.at[(core + n) % 2, (zl + n // 2) % 2]
-        return remote(share, pair_in.at[n], pair_send.at[n], pair_recv.at[n], quad(n))
-
-    for n in (3, 2, 1):
-        pair_copy(n).start()
-
     half32[:, 0:24] = turned.astype(F32).T
 
     lane = lax.broadcasted_iota(jnp.int32, (16, 128), 1)
@@ -148,14 +138,27 @@
         for n in range(3):
             rows_out[zz, :, n * 128 : n * 128 + 128] = tiles[n].astype(BF16)
 
+    pl.semaphore_wait(barrier, 47)
+
+    def pair_copy(n):
+        share = part32.at[(core + n) % 2, (zl + n // 2) % 2]
+        return remote(share, pair_in.at[n], pair_send.at[n], pair_recv.at[n], quad(n))
+
+    for n in (3, 2, 1):
+        pair_copy(n).start()
+
     def rows_copy(k):
         to = (zh + k) % 4
         device = (x * 16 + to * 4 + y, orb)
         return remote(rows_out.at[to], rows_in.at[k], rows_send.at[k], rows_recv.at[k], device)
 
-    @pl.loop(1, 4)
-    def _(k):
-        rows_copy(k).start()
+    @pl.loop(0, 4)
+    def _(n):
+        k = (n - zh + 4) % 4
+
+        @pl.when(k != 0)
+        def _():
+            rows_copy(k).start()
 
     for n in (1, 2, 3):
         pair_copy(n).wait_recv()
@@ -265,6 +268,22 @@
     for n in (1, 2, 3):
         pair_copy(n).wait_send()
 
+    @pl.when(jnp.logical_not(origin))
+    def _():
+        for n in range(2):
+
+            @pl.loop(n * 8 + 1 - n, n * 8 + 8)
+            def _(k):
+                block_copy(2 * k, core).wait_recv()
+
+            share_copy(n, core).start()
+
+    @pl.loop(1, 16)
+    def _(k):
+        turn_copy(k).wait_recv()
+
+    own = turn_in[...].reshape(256, 128).astype(F32).T[0:96].astype(BF16)
+
     @pl.when(origin)
     def _():
         @pl.loop(1, 16)
@@ -277,23 +296,10 @@
     @pl.when(jnp.logical_not(origin))
     def _():
         for n in range(2):
-
-            @pl.loop(n * 8 + 1 - n, n * 8 + 8)
-            def _(k):
-                block_copy(2 * k, core).wait_recv()
-
-            share_copy(n, core).start()
-
-        for n in range(2):
             share_copy(n, 1 - core).wait_recv()
 
-    @pl.loop(1, 16)
-    def _(k):
-        turn_copy(k).wait_recv()
-
-    own = turn_in[...].reshape(256, 128)[:, 0:96]
-    first = lax.dot_general(own, gathered[0].reshape(256, 384), TN, preferred_element_type=F32)
-    second = lax.dot_general(own, gathered[1].reshape(256, 384), TN, preferred_element_type=F32)
+    first = jnp.dot(own, gathered[0].reshape(256, 384), preferred_element_type=F32)
+    second = jnp.dot(own, gathered[1].reshape(256, 384), preferred_element_type=F32)
     lane = lax.broadcasted_iota(jnp.int32, (96, 128), 1)
     a, b, c = (pltpu.roll(second[:, n * 128 : n * 128 + 128], 32, 1) for n in range(3))
     tiles = (
@@ -331,15 +337,18 @@
     tile = ints[...].reshape(96, 576)
     high = tile.astype(BF16)
     split[0:96, :] = high
-    split[96:192, :] = (tile - high.astype(F32)).astype(BF16)
-
-    pairs = lax.dot_general(split[...], density[...], NT, preferred_element_type=F32)
-    pairs = pairs[0:96] + pairs[96:192]
-    row = lax.broadcasted_iota(jnp.int32, (96, 576), 0) % 24
-    col = lax.broadcasted_iota(jnp.int32, (96, 576), 1) % 24
-    kept = jnp.where(row == col, pairs, 0.0).reshape(4, 24, 576).sum(axis=1)
-    pick = lax.broadcasted_iota(jnp.int32, (576, 24), 0) // 24 == lax.broadcasted_iota(jnp.int32, (576, 24), 1)
-    fock[...] = jnp.dot(kept, pick.astype(F32), precision=lax.Precision.HIGHEST, preferred_element_type=F32)
+    split[96:128, :] = jnp.zeros((32, 576), BF16)
+    split[128:224, :] = (tile - high.astype(F32)).astype(BF16)
+
+    pairs = lax.dot_general(density[...], split[...], NT, preferred_element_type=F32)
+    pairs = pairs[:, 0:96] + pairs[:, 128:224]
+    row = lax.broadcasted_iota(jnp.int32, (576, 96), 0) % 24
+    col = lax.broadcasted_iota(jnp.int32, (576, 96), 1) % 24
+    kept = jnp.where(row == col, pairs, 0.0).reshape(24, 24, 96).sum(axis=1)
+    pick = lax.broadcasted_iota(jnp.int32, (4, 96), 0) == lax.broadcasted_iota(jnp.int32, (4, 96), 1) // 24
+    fock[...] = lax.dot_general(
+        pick.astype(F32), kept, NT, precision=lax.Precision.HIGHEST, preferred_element_type=F32
+    )
     copy.wait()
 
 
@@ -383,7 +392,7 @@
         out_shape=(jax.ShapeDtypeStruct((4, 24, 576), F32), jax.ShapeDtypeStruct((4, 24), F32)),
         in_specs=[vmem, vmem],
         out_specs=(hbm, vmem),
-        scratch_shapes=[pltpu.VMEM((192, 576), BF16), dma],
+        scratch_shapes=[pltpu.VMEM((224, 576), BF16), dma],
         compiler_params=pltpu.CompilerParams(vmem_limit_bytes=16 * 2**20),
     )(ints, pair_density.reshape(576, 576))
 

time: 36 us -> 35.8 us (level)
  no operation moved by 1% of the time
where the time goes in v6:
time: 35.8 us; the launch traced here: 35.7 us
  Pallas kernels  35.1 us (98%)
  between operations  0.65 us (2%)
    pallas_call x1, Pallas kernels, shards(): pl.pallas_call(kernel, name='half_active_fock', out_shape=jax.ShapeDtypeS...  33.7 us
    pallas_call x1, Pallas kernels, shards(): pl.pallas_call(fock_kernel, name='fock', out_shape=(jax.ShapeDtypeStruct(...  1.35 us

profile of v6, /device:TPU:1, one launch (start us, length us, event | category | flops | bytes accessed | tf_op | source)
XLA Modules:
  0.0 35.7 jit_solution(7496478470504003081)
XLA Ops:
  0.6 0.0 copy-start
  0.6 33.7 %half_active_fock.1.ints = f32[4,24,576]{2,1,0:T(8,128)S(1)} custom-call(bf16[4,256,2048]{2,1,0:T(8,128)(2,1)} %chol.1, bf16[24,2048]{1,0:T(8,128)(2,1)} %bitcast.3), custom_call_target="tpu_custom_call" | custom-call | tf_op jit(solution)/shard_map/half_active_fock/pallas_call | solution.py:359
  34.4 0.0 copy-done
  34.4 1.3 %fock.1 = (f32[4,24,576]{2,1,0:T(8,128)}, f32[4,24]{1,0:T(4,128)}) custom-call(f32[4,24,576]{2,1,0:T(8,128)S(1)} %half_active_fock.1.ints, bf16[576,576]{1,0:T(8,128)(2,1)S(1)} %bitcast.2), custom_call_target="tpu_custom_call" | custom-call | tf_op jit(solution)/shard_map/fock/pallas_call | solution.py:389
Async XLA Ops:
  0.6 33.7 %copy-start = (bf16[24,24,576]{2,1,0:T(8,128)(2,1)S(1)}, bf16[24,24,576]{2,1,0:T(8,128)(2,1)}, u32[]{:S(2)}) copy-start(bf16[24,24,576]{2,1,0:T(8,128)(2,1)} %param.5) | copy-start | bytes 1990660

commit v7 on v6

--- a/solution.py
+++ b/solution.py
@@ -62,7 +62,7 @@
 
     barrier = pltpu.get_barrier_semaphore()
 
-    @pl.loop(0, 16)
+    @pl.loop(0, 16, unroll=True)
     def _(n):
         k = column_to(n)
 
@@ -73,7 +73,7 @@
     pl.semaphore_signal(barrier, inc=1, device_id=sibling, device_id_type=MESH)
     pl.semaphore_signal(barrier, inc=1, device_id=quad(3), device_id_type=MESH)
 
-    @pl.loop(0, 16)
+    @pl.loop(0, 16, unroll=True)
     def _(n):
         k = plane_to(n)
 
@@ -152,7 +152,7 @@
         device = (x * 16 + to * 4 + y, orb)
         return remote(rows_out.at[to], rows_in.at[k], rows_send.at[k], rows_recv.at[k], device)
 
-    @pl.loop(0, 4)
+    @pl.loop(0, 4, unroll=True)
     def _(n):
         k = (n - zh + 4) % 4
 
@@ -169,7 +169,7 @@
     def part_copy(k):
         return remote(part_out, part_in.at[k], part_send.at[k], part_recv.at[k], column(k))
 
-    @pl.loop(0, 16)
+    @pl.loop(0, 16, unroll=True)
     def _(n):
         k = column_to(n)
 
@@ -179,7 +179,7 @@
 
     rows_in[0] = rows_out[zh]
 
-    @pl.loop(1, 4)
+    @pl.loop(1, 4, unroll=True)
     def _(k):
         rows_copy(k).wait_recv()
 
@@ -201,7 +201,7 @@
         to = ((x + k // 4) % 4) * 4 + (y + k % 4) % 4
         return remote(turn_out.at[to], turn_in.at[k], turn_send.at[k], turn_recv.at[k], plane(k))
 
-    @pl.loop(0, 16)
+    @pl.loop(0, 16, unroll=True)
     def _(n):
         k = plane_to(n)
 
@@ -211,7 +211,7 @@
 
     turn_in[0] = turn_out[x * 4 + y]
 
-    @pl.loop(1, 16)
+    @pl.loop(1, 16, unroll=True)
     def _(k):
         part_copy(k).wait_recv()
 
@@ -249,7 +249,7 @@
     def _():
         block_copy(1, core).start()
 
-    @pl.loop(1, 16)
+    @pl.loop(1, 16, unroll=True)
     def _(n):
         k = plane_to(n)
 
@@ -257,11 +257,11 @@
         def _():
             block_copy(2 * k, core).start()
 
-    @pl.loop(1, 16)
+    @pl.loop(1, 16, unroll=True)
     def _(k):
         part_copy(k).wait_send()
 
-    @pl.loop(1, 4)
+    @pl.loop(1, 4, unroll=True)
     def _(k):
         rows_copy(k).wait_send()
 
@@ -272,13 +272,13 @@
     def _():
         for n in range(2):
 
-            @pl.loop(n * 8 + 1 - n, n * 8 + 8)
+            @pl.loop(n * 8 + 1 - n, n * 8 + 8, unroll=True)
             def _(k):
                 block_copy(2 * k, core).wait_recv()
 
             share_copy(n, core).start()
 
-    @pl.loop(1, 16)
+    @pl.loop(1, 16, unroll=True)
     def _(k):
         turn_copy(k).wait_recv()
 
@@ -286,7 +286,7 @@
 
     @pl.when(origin)
     def _():
-        @pl.loop(1, 16)
+        @pl.loop(1, 16, unroll=True)
         def _(k):
             block_copy(2 * k, core).wait_recv()
             block_copy(2 * k, 1 - core).wait_recv()
@@ -325,7 +325,7 @@
             share_copy(n, core).wait_send()
 
 
-    @pl.loop(1, 16)
+    @pl.loop(1, 16, unroll=True)
     def _(k):
         turn_copy(k).wait_send()
         block_copy(2 * k, core).wait_send()

time: 35.8 us -> 35.7 us (level)
  Pallas kernels: 35.1 us -> 34.7 us
    pallas_call x1, Pallas kernels: 33.7 us -> 33.3 us  [shards(): pl.pallas_call(kernel, name='half_active_fock', out_shape=jax.ShapeDtypeS...]
where the time goes in v7:
time: 35.7 us; the launch traced here: 35.3 us
  Pallas kernels  34.7 us (97%)
  between operations  0.65 us (2%)
    pallas_call x1, Pallas kernels, shards(): pl.pallas_call(kernel, name='half_active_fock', out_shape=jax.ShapeDtypeS...  33.3 us
    pallas_call x1, Pallas kernels, shards(): pl.pallas_call(fock_kernel, name='fock', out_shape=(jax.ShapeDtypeStruct(...  1.35 us

profile of v7, /device:TPU:1, one launch (start us, length us, event | category | flops | bytes accessed | tf_op | source)
XLA Modules:
  0.0 35.3 jit_solution(6546704181051400695)
XLA Ops:
  0.6 0.0 copy-start
  0.6 33.3 %half_active_fock.1.ints = f32[4,24,576]{2,1,0:T(8,128)S(1)} custom-call(bf16[4,256,2048]{2,1,0:T(8,128)(2,1)} %chol.1, bf16[24,2048]{1,0:T(8,128)(2,1)} %bitcast.3), custom_call_target="tpu_custom_call" | custom-call | tf_op jit(solution)/shard_map/half_active_fock/pallas_call | solution.py:359
  34.0 0.0 copy-done
  34.0 1.3 %fock.1 = (f32[4,24,576]{2,1,0:T(8,128)}, f32[4,24]{1,0:T(4,128)}) custom-call(f32[4,24,576]{2,1,0:T(8,128)S(1)} %half_active_fock.1.ints, bf16[576,576]{1,0:T(8,128)(2,1)S(1)} %bitcast.2), custom_call_target="tpu_custom_call" | custom-call | tf_op jit(solution)/shard_map/fock/pallas_call | solution.py:389
Async XLA Ops:
  0.6 33.4 %copy-start = (bf16[24,24,576]{2,1,0:T(8,128)(2,1)S(1)}, bf16[24,24,576]{2,1,0:T(8,128)(2,1)}, u32[]{:S(2)}) copy-start(bf16[24,24,576]{2,1,0:T(8,128)(2,1)} %param.5) | copy-start | bytes 1990660

commit v8 on v7

--- a/solution.py
+++ b/solution.py
@@ -235,7 +235,7 @@
         return remote(block_out, there, block_send.at[n], block_recv.at[source, n // 2], chips(n))
 
     def share_copy(n, source):
-        there = gathered.at[source, pl.ds(n * 8, 8)]
+        there = gathered.at[source, pl.ds(n * 4, 4)]
         return remote(there, there, share_send.at[n], share_recv.at[n], sibling)
 
     first_k = plane_to(0)
@@ -270,9 +270,9 @@
 
     @pl.when(jnp.logical_not(origin))
     def _():
-        for n in range(2):
-
-            @pl.loop(n * 8 + 1 - n, n * 8 + 8, unroll=True)
+        for n in range(4):
+
+            @pl.loop(max(n * 4, 1), n * 4 + 4, unroll=True)
             def _(k):
                 block_copy(2 * k, core).wait_recv()
 
@@ -295,7 +295,7 @@
 
     @pl.when(jnp.logical_not(origin))
     def _():
-        for n in range(2):
+        for n in range(4):
             share_copy(n, 1 - core).wait_recv()
 
     first = jnp.dot(own, gathered[0].reshape(256, 384), preferred_element_type=F32)
@@ -321,7 +321,7 @@
     @pl.when(jnp.logical_not(origin))
     def _():
         block_copy(2 * first_k + 1, core).wait_send()
-        for n in range(2):
+        for n in range(4):
             share_copy(n, core).wait_send()
 
 
@@ -380,7 +380,7 @@
             pltpu.VMEM((16, 384), BF16),
             pltpu.VMEM((2, 16, 16, 384), BF16),
             dma((len(CUTS) - 1,)), dma, dma((4,)), dma((4,)), dma((4,)), dma((4,)), dma((16,)), dma((16,)),
-            dma((16,)), dma((16,)), dma((32,)), dma((2, 16)), dma((2,)), dma((2,)),
+            dma((16,)), dma((16,)), dma((32,)), dma((2, 16)), dma((4,)), dma((4,)),
         ],
         compiler_params=pltpu.CompilerParams(
             collective_id=0, has_side_effects=True, vmem_limit_bytes=16 * 2**20

time: 35.7 us -> 35.7 us (level)
  no operation moved by 1% of the time
where the time goes in v8:
time: 35.7 us; the launch traced here: 35.4 us
  Pallas kernels  34.7 us (97%)
  between operations  0.65 us (2%)
    pallas_call x1, Pallas kernels, shards(): pl.pallas_call(kernel, name='half_active_fock', out_shape=jax.ShapeDtypeS...  33.4 us
    pallas_call x1, Pallas kernels, shards(): pl.pallas_call(fock_kernel, name='fock', out_shape=(jax.ShapeDtypeStruct(...  1.35 us

profile of v8, /device:TPU:1, one launch (start us, length us, event | category | flops | bytes accessed | tf_op | source)
XLA Modules:
  0.0 35.4 jit_solution(16086192357244299573)
XLA Ops:
  0.6 0.0 copy-start
  0.6 33.4 %half_active_fock.1.ints = f32[4,24,576]{2,1,0:T(8,128)S(1)} custom-call(bf16[4,256,2048]{2,1,0:T(8,128)(2,1)} %chol.1, bf16[24,2048]{1,0:T(8,128)(2,1)} %bitcast.3), custom_call_target="tpu_custom_call" | custom-call | tf_op jit(solution)/shard_map/half_active_fock/pallas_call | solution.py:359
  34.0 0.0 copy-done
  34.0 1.3 %fock.1 = (f32[4,24,576]{2,1,0:T(8,128)}, f32[4,24]{1,0:T(4,128)}) custom-call(f32[4,24,576]{2,1,0:T(8,128)S(1)} %half_active_fock.1.ints, bf16[576,576]{1,0:T(8,128)(2,1)S(1)} %bitcast.2), custom_call_target="tpu_custom_call" | custom-call | tf_op jit(solution)/shard_map/fock/pallas_call | solution.py:389
Async XLA Ops:
  0.6 33.4 %copy-start = (bf16[24,24,576]{2,1,0:T(8,128)(2,1)S(1)}, bf16[24,24,576]{2,1,0:T(8,128)(2,1)}, u32[]{:S(2)}) copy-start(bf16[24,24,576]{2,1,0:T(8,128)(2,1)} %param.5) | copy-start | bytes 1990660
